TPU v7x, 32 devices: a whole 2x2x4 slice. The times are simulated.
32 devices in a mesh: dp: 16 (over z, x, core), mp: 2 (over y).
Axes of the slice: x: 2, y: 2, z: 4, core: 2. Of those that a mesh axis runs over, the one named last changes fastest.
Arguments:
- images: bfloat16 [64, 196, 512], P('dp'), may hold values from -6 to 6
- cotangent: bfloat16 [64, 196, 512], P('dp'), may hold values from -6 to 6
- w_query: bfloat16 [512, 512], P('dp', 'mp'), may hold values from -0.25 to 0.25
- w_key: bfloat16 [512, 512], P('dp', 'mp'), may hold values from -0.25 to 0.25
- w_value: bfloat16 [512, 512], P('dp', 'mp'), may hold values from -0.25 to 0.25
- w_proj: bfloat16 [512, 512], P('mp', 'dp'), may hold values from -1 to 1
- w_up: bfloat16 [512, 2048], P('dp', 'mp'), may hold values from -0.25 to 0.25
- w_down: bfloat16 [2048, 512], P('mp', 'dp'), may hold values from -0.125 to 0.125
- gains: bfloat16 [2, 512], P(None, 'dp'), may hold values from 0.25 to 1.75
- shifts: bfloat16 [4, 512], P(None, 'dp'), may hold values from -3 to 3
- qv_bias: bfloat16 [2, 512], P(None, 'mp'), may hold values from -3 to 3
- up_bias: bfloat16 [2048], P('mp'), may hold values from -3 to 3
- table: bfloat16 [16, 169], P('mp'), may hold values from -5 to 5
- regions: int32 [4, 49], replicated, may hold values from 0 to 3
- rel_index: int32 [49, 49], replicated, may hold values from 0 to 168
Outputs:
- output: bfloat16 [64, 196, 512], P('dp')
- d_images: bfloat16 [64, 196, 512], P('dp')
- g_query: float32 [512, 512], P('dp', 'mp')
- g_key: float32 [512, 512], P('dp', 'mp')
- g_value: float32 [512, 512], P('dp', 'mp')
- g_proj: float32 [512, 512], P('mp', 'dp')
- g_up: float32 [512, 2048], P('dp', 'mp')
- g_down: float32 [2048, 512], P('mp', 'dp')
- g_gains: float32 [2, 512], P(None, 'dp')
- g_shifts: float32 [4, 512], P(None, 'dp')
- g_qv_bias: float32 [2, 512], P(None, 'mp')
- g_up_bias: float32 [2048], P('mp')
- g_table: float32 [16, 169], P('mp')
Inputs may be any that keep to these rules, and one draw needn't show every extreme that they name: `regions`: a position's scores to positions of another region of its window get -100.
All inputs are finite; a program needn't handle non-finite values.
Results may differ from a plain program's by a relative error of at most 0.017.
Values may be sent and summed in bfloat16 or wider, within the bound.
No kernel may reach another device: no remote copies, remote signals or barrier semaphores. Data moves between devices by JAX's collectives and lax.ppermute only.
A program may use at most 128 MiB of HBM per device.

v0:
```python
import math
import jax
import jax.numpy as jnp
from jax import lax
from jax.sharding import PartitionSpec as P

HEAD_DIM = 32
SIDE = 14
WIN = 7
SHIFT = 3
MICRO = 2
WINDOWS = 4


def to_windows(source):
    image_count = source.shape[0]
    channels = source.shape[2]
    grid = source.reshape(image_count, SIDE, SIDE, channels)
    grid = jnp.roll(grid, (-SHIFT, -SHIFT), (1, 2))
    grid = grid.reshape(image_count, SIDE // WIN, WIN, SIDE // WIN, WIN, channels)
    return grid.transpose(0, 1, 3, 2, 4, 5).reshape(image_count * WINDOWS, WIN * WIN, channels)


def from_windows(source, image_count):
    channels = source.shape[2]
    grid = source.reshape(image_count, SIDE // WIN, SIDE // WIN, WIN, WIN, channels)
    grid = grid.transpose(0, 1, 3, 2, 4, 5).reshape(image_count, SIDE, SIDE, channels)
    grid = jnp.roll(grid, (SHIFT, SHIFT), (1, 2))
    return grid.reshape(image_count, SIDE * SIDE, channels)


def normalize(source, gain_row, shift_row):
    centred = source - jnp.mean(source, axis=-1, keepdims=True)
    inverse = lax.rsqrt(jnp.mean(centred * centred, axis=-1, keepdims=True) + 1e-05)
    unit_rows = centred * inverse
    return (unit_rows * gain_row + shift_row, unit_rows, inverse)


def norm_back(grad_in, unit_rows, inverse, gain_row):
    scaled = grad_in * gain_row
    return inverse * (
        scaled
        - jnp.mean(scaled, axis=-1, keepdims=True)
        - unit_rows * jnp.mean(scaled * unit_rows, axis=-1, keepdims=True)
    )


def gelu_slope(hidden):
    normal_cdf = 0.5 * (1.0 + lax.erf(hidden * (1.0 / math.sqrt(2.0))))
    density = jnp.exp(-0.5 * hidden * hidden) * (1.0 / math.sqrt(2.0 * math.pi))
    return normal_cdf + hidden * density


def inner(left_mat, right_mat):
    return lax.dot_general(
        left_mat, right_mat, (((0,), (0,)), ((), ())), preferred_element_type=jnp.float32
    )


def against(left_mat, right_mat):
    return lax.dot_general(
        left_mat, right_mat, (((1,), (1,)), ((), ())), preferred_element_type=jnp.float32
    )


def body(
    images,
    cotangent,
    w_query,
    w_key,
    w_value,
    w_proj,
    w_up,
    w_down,
    gains,
    shifts,
    qv_bias,
    up_bias,
    table,
    regions,
    rel_index,
):
    image_count = images.shape[0] // MICRO
    row_count = image_count * SIDE * SIDE
    model_width = images.shape[2]
    local_width = qv_bias.shape[1]
    local_heads = table.shape[0]
    up_width = up_bias.shape[0]
    window_tokens = regions.shape[1]
    window_count = image_count * WINDOWS
    score_scale = HEAD_DIM ** (-0.5)
    table_codes = jnp.arange(table.shape[1], dtype=jnp.int32)
    onehot = (rel_index.reshape(1, -1) == table_codes[:, None]).astype(jnp.float32)
    rel_bias = jnp.dot(table.astype(jnp.float32), onehot, precision=lax.Precision.HIGHEST).reshape(
        local_heads, window_tokens, window_tokens
    )
    region_mask = jnp.where(regions[:, :, None] == regions[:, None, :], 0.0, -100.0).astype(
        jnp.float32
    )
    query_bias = qv_bias[0].astype(jnp.float32)
    value_bias = qv_bias[1].astype(jnp.float32)
    up_float = up_bias.astype(jnp.float32)

    def logits_of(query_heads, key_heads):
        raw = (
            jnp.einsum(
                "wihd,wjhd->whij", query_heads, key_heads, preferred_element_type=jnp.float32
            )
            * score_scale
        )
        framed = raw.reshape(image_count, WINDOWS, local_heads, window_tokens, window_tokens)
        framed = framed + region_mask[None, :, None] + rel_bias[None, None]
        return framed.reshape(window_count, local_heads, window_tokens, window_tokens)

    acc_query = jnp.zeros((model_width, local_width), jnp.float32)
    acc_key = jnp.zeros((model_width, local_width), jnp.float32)
    acc_value = jnp.zeros((model_width, local_width), jnp.float32)
    acc_proj = jnp.zeros((local_width, model_width), jnp.float32)
    acc_up = jnp.zeros((model_width, up_width), jnp.float32)
    acc_down = jnp.zeros((up_width, model_width), jnp.float32)
    gain_acc = jnp.zeros((2, model_width), jnp.float32)
    shift_acc = jnp.zeros((4, model_width), jnp.float32)
    table_acc = jnp.zeros(table.shape, jnp.float32)
    qv_acc = jnp.zeros(qv_bias.shape, jnp.float32)
    up_bias_acc = jnp.zeros(up_bias.shape, jnp.float32)
    outputs_list = []
    input_grads = []
    for micro_step in range(MICRO):
        ahead = (
            lax.all_gather(w_query, "dp", axis=0, tiled=True),
            lax.all_gather(w_key, "dp", axis=0, tiled=True),
            lax.all_gather(w_value, "dp", axis=0, tiled=True),
            lax.all_gather(w_proj, "dp", axis=1, tiled=True),
            lax.all_gather(w_up, "dp", axis=0, tiled=True),
            lax.all_gather(w_down, "dp", axis=1, tiled=True),
            lax.all_gather(gains, "dp", axis=1, tiled=True),
            lax.all_gather(shifts, "dp", axis=1, tiled=True),
        )
        full_query, full_key, full_value, full_proj, full_up, full_down, full_gains, full_shifts = (
            ahead
        )
        gain_rows = full_gains.astype(jnp.float32)
        shift_rows = full_shifts.astype(jnp.float32)
        first_row = micro_step * image_count
        source = images[first_row : first_row + image_count].astype(jnp.float32)
        normed_one, unit_one, inverse_one = normalize(source, gain_rows[0], shift_rows[0])
        window_rows = to_windows(normed_one.astype(jnp.bfloat16)).reshape(row_count, model_width)
        queries = (
            jnp.dot(window_rows, full_query, preferred_element_type=jnp.float32) + query_bias
        ).astype(jnp.bfloat16)
        key_rows = jnp.dot(window_rows, full_key, preferred_element_type=jnp.float32).astype(
            jnp.bfloat16
        )
        values = (
            jnp.dot(window_rows, full_value, preferred_element_type=jnp.float32) + value_bias
        ).astype(jnp.bfloat16)
        query_heads = queries.reshape(window_count, window_tokens, local_heads, HEAD_DIM)
        key_heads = key_rows.reshape(window_count, window_tokens, local_heads, HEAD_DIM)
        value_heads = values.reshape(window_count, window_tokens, local_heads, HEAD_DIM)
        logits = logits_of(query_heads, key_heads)
        row_max = jnp.max(logits, axis=-1, keepdims=True)
        log_total = row_max + jnp.log(jnp.sum(jnp.exp(logits - row_max), axis=-1, keepdims=True))
        soft_low = jnp.exp(logits - log_total).astype(jnp.bfloat16)
        mixed_out = jnp.einsum(
            "whij,wjhd->wihd", soft_low, value_heads, preferred_element_type=jnp.float32
        ).astype(jnp.bfloat16)
        token_mixed = from_windows(
            mixed_out.reshape(window_count, window_tokens, local_width), image_count
        ).reshape(row_count, local_width)
        projected = jnp.dot(token_mixed, full_proj, preferred_element_type=jnp.float32)
        source_rows = source.reshape(row_count, model_width)
        branch = lax.psum(projected, "mp") + shift_rows[2]
        middle = source_rows + branch
        normed_two, unit_two, inverse_two = normalize(middle, gain_rows[1], shift_rows[1])
        normed_low = normed_two.astype(jnp.bfloat16)
        hidden = jnp.dot(normed_low, full_up, preferred_element_type=jnp.float32) + up_float
        active = jax.nn.gelu(hidden, approximate=False).astype(jnp.bfloat16)
        lowered = jnp.dot(active, full_down, preferred_element_type=jnp.float32)
        outward = lax.psum(lowered.astype(jnp.bfloat16), "mp").astype(jnp.float32) + shift_rows[3]
        finished = (middle + outward).astype(jnp.bfloat16)
        outputs_list.append(finished.reshape(source.shape))
        behind = (
            lax.all_gather(w_query, "dp", axis=0, tiled=True),
            lax.all_gather(w_key, "dp", axis=0, tiled=True),
            lax.all_gather(w_value, "dp", axis=0, tiled=True),
            lax.all_gather(w_proj, "dp", axis=1, tiled=True),
            lax.all_gather(w_up, "dp", axis=0, tiled=True),
            lax.all_gather(w_down, "dp", axis=1, tiled=True),
            lax.all_gather(gains, "dp", axis=1, tiled=True),
            lax.all_gather(shifts, "dp", axis=1, tiled=True),
        )
        back_query, back_key, back_value, back_proj, back_up, back_down, back_gains, back_shifts = (
            behind
        )
        back_gain_rows = back_gains.astype(jnp.float32)
        grad_low = cotangent[first_row : first_row + image_count].reshape(row_count, model_width)
        grad_out = grad_low.astype(jnp.float32)
        acc_down = acc_down + inner(active, grad_low)
        grad_hidden = (against(grad_low, back_down) * gelu_slope(hidden)).astype(jnp.bfloat16)
        up_bias_acc = up_bias_acc + jnp.sum(grad_hidden.astype(jnp.float32), axis=0)
        acc_up = acc_up + inner(normed_low, grad_hidden)
        lifted = against(grad_hidden, back_up)
        grad_normed_two = lax.psum(lifted, "mp")
        shift_acc = shift_acc.at[3].add(jnp.sum(grad_out, axis=0))
        gain_acc = gain_acc.at[1].add(jnp.sum(grad_normed_two * unit_two, axis=0))
        shift_acc = shift_acc.at[1].add(jnp.sum(grad_normed_two, axis=0))
        grad_middle = grad_out + norm_back(
            grad_normed_two, unit_two, inverse_two, back_gain_rows[1]
        )
        shift_acc = shift_acc.at[2].add(jnp.sum(grad_middle, axis=0))
        grad_branch = grad_middle.astype(jnp.bfloat16)
        acc_proj = acc_proj + inner(token_mixed, grad_branch)
        grad_token = against(grad_branch, back_proj).astype(jnp.bfloat16)
        grad_mixed = to_windows(grad_token.reshape(image_count, SIDE * SIDE, local_width)).reshape(
            window_count, window_tokens, local_heads, HEAD_DIM
        )
        soft_again = jnp.exp(logits_of(query_heads, key_heads) - log_total)
        soft_again_low = soft_again.astype(jnp.bfloat16)
        grad_values = (
            jnp.einsum(
                "whij,wihd->wjhd", soft_again_low, grad_mixed, preferred_element_type=jnp.float32
            )
            .astype(jnp.bfloat16)
            .reshape(row_count, local_width)
        )
        grad_soft = jnp.einsum(
            "wihd,wjhd->whij", grad_mixed, value_heads, preferred_element_type=jnp.float32
        )
        grad_logits = soft_again * (
            grad_soft - jnp.sum(grad_soft * soft_again, axis=-1, keepdims=True)
        )
        table_acc = table_acc + jnp.dot(
            jnp.sum(grad_logits, axis=0).reshape(local_heads, -1),
            onehot.T,
            precision=lax.Precision.HIGHEST,
        )
        grad_scores = grad_logits.astype(jnp.bfloat16)
        grad_queries = (
            (
                jnp.einsum(
                    "whij,wjhd->wihd", grad_scores, key_heads, preferred_element_type=jnp.float32
                )
                * score_scale
            )
            .astype(jnp.bfloat16)
            .reshape(row_count, local_width)
        )
        grad_keys = (
            (
                jnp.einsum(
                    "whij,wihd->wjhd", grad_scores, query_heads, preferred_element_type=jnp.float32
                )
                * score_scale
            )
            .astype(jnp.bfloat16)
            .reshape(row_count, local_width)
        )
        qv_acc = qv_acc + jnp.stack(
            [
                jnp.sum(grad_queries.astype(jnp.float32), axis=0),
                jnp.sum(grad_values.astype(jnp.float32), axis=0),
            ]
        )
        acc_query = acc_query + inner(window_rows, grad_queries)
        acc_key = acc_key + inner(window_rows, grad_keys)
        acc_value = acc_value + inner(window_rows, grad_values)
        grad_window = (
            against(grad_queries, back_query)
            + against(grad_keys, back_key)
            + against(grad_values, back_value)
        )
        token_terms = from_windows(
            grad_window.reshape(window_count, window_tokens, model_width), image_count
        ).reshape(row_count, model_width)
        unit_one_rows = unit_one.reshape(row_count, model_width)
        inverse_rows = inverse_one.reshape(row_count, 1)
        grad_normed_one = lax.psum(token_terms, "mp")
        gain_acc = gain_acc.at[0].add(jnp.sum(grad_normed_one * unit_one_rows, axis=0))
        shift_acc = shift_acc.at[0].add(jnp.sum(grad_normed_one, axis=0))
        grad_source = grad_middle + norm_back(
            grad_normed_one, unit_one_rows, inverse_rows, back_gain_rows[0]
        )
        finished_grad = grad_source.astype(jnp.bfloat16)
        input_grads.append(finished_grad.reshape(source.shape))
    owned = (
        lax.psum_scatter(
            acc_query.astype(jnp.bfloat16), "dp", scatter_dimension=0, tiled=True
        ).astype(jnp.float32),
        lax.psum_scatter(
            acc_key.astype(jnp.bfloat16), "dp", scatter_dimension=0, tiled=True
        ).astype(jnp.float32),
        lax.psum_scatter(
            acc_value.astype(jnp.bfloat16), "dp", scatter_dimension=0, tiled=True
        ).astype(jnp.float32),
        lax.psum_scatter(
            acc_proj.astype(jnp.bfloat16), "dp", scatter_dimension=1, tiled=True
        ).astype(jnp.float32),
        lax.psum_scatter(acc_up.astype(jnp.bfloat16), "dp", scatter_dimension=0, tiled=True).astype(
            jnp.float32
        ),
        lax.psum_scatter(
            acc_down.astype(jnp.bfloat16), "dp", scatter_dimension=1, tiled=True
        ).astype(jnp.float32),
        lax.psum_scatter(
            gain_acc.astype(jnp.bfloat16), "dp", scatter_dimension=1, tiled=True
        ).astype(jnp.float32),
        lax.psum_scatter(
            shift_acc.astype(jnp.bfloat16), "dp", scatter_dimension=1, tiled=True
        ).astype(jnp.float32),
    )
    head_sums = lax.psum((table_acc, qv_acc, up_bias_acc), "dp")
    return (
        jnp.concatenate(outputs_list, axis=0),
        jnp.concatenate(input_grads, axis=0),
        owned[0],
        owned[1],
        owned[2],
        owned[3],
        owned[4],
        owned[5],
        owned[6],
        owned[7],
        head_sums[1],
        head_sums[2],
        head_sums[0],
    )


def solution(mesh):
    return jax.shard_map(
        body,
        mesh=mesh,
        in_specs=(
            P("dp", None, None),
            P("dp", None, None),
            P("dp", "mp"),
            P("dp", "mp"),
            P("dp", "mp"),
            P("mp", "dp"),
            P("dp", "mp"),
            P("mp", "dp"),
            P(None, "dp"),
            P(None, "dp"),
            P(None, "mp"),
            P("mp"),
            P("mp", None),
            P(),
            P(),
        ),
        out_specs=(
            P("dp", None, None),
            P("dp", None, None),
            P("dp", "mp"),
            P("dp", "mp"),
            P("dp", "mp"),
            P("mp", "dp"),
            P("dp", "mp"),
            P("mp", "dp"),
            P(None, "dp"),
            P(None, "dp"),
            P(None, "mp"),
            P("mp"),
            P("mp", None),
        ),
        check_vma=False,
    )
```

profile of v0, /device:TPU:0, one launch (start us, length us, event | category | flops | bytes accessed | tf_op | source)
XLA Modules:
  0.0 806.4 jit_solution(6925962472406569646)
XLA Ops:
  8.1 23.4 %all-gather = bf16[16,32,2]{1,2,0:T(2,128)(2,1)S(1)} all-gather(bf16[1,32,2]{1,2,0:T(2,128)(2,1)} %bitcast.263), channel_id=1, replica_groups=mesh['dp'=16,'mp'=2] {'dp'}, dimensions={0}, use_global_device_ids=true | all-gather | bytes 2176 | tf_op jit(solution)/shard_map/all_gather | solution.py:136
  31.6 17.7 %all-gather.1 = bf16[16,32,4]{1,2,0:T(4,128)(2,1)S(1)} all-gather(bf16[1,32,4]{1,2,0:T(4,128)(2,1)} %bitcast.262), channel_id=1, replica_groups=mesh['dp'=16,'mp'=2] {'dp'}, dimensions={0}, use_global_device_ids=true | all-gather | bytes 4352 | tf_op jit(solution)/shard_map/all_gather | solution.py:137
  54.4 2.8 subtract_multiply_fusion.4
  57.9 19.4 %all_gather.19 = bf16[512,256]{1,0:T(8,128)(2,1)S(1)} all-gather(bf16[32,256]{1,0:T(8,128)(2,1)S(1)} %copy-done.61), channel_id=1, replica_groups=mesh['dp'=16,'mp'=2] {'dp'}, dimensions={0}, use_global_device_ids=true | all-gather | bytes 278528 | tf_op jit(solution)/shard_map/all_gather | solution.py:130
  77.4 18.2 %all_gather.18 = bf16[512,256]{1,0:T(8,128)(2,1)S(1)} all-gather(bf16[32,256]{1,0:T(8,128)(2,1)S(1)} %copy-done.62), channel_id=1, replica_groups=mesh['dp'=16,'mp'=2] {'dp'}, dimensions={0}, use_global_device_ids=true | all-gather | bytes 278528 | tf_op jit(solution)/shard_map/all_gather | solution.py:132
  100.4 19.6 %all_gather.20 = bf16[512,256]{1,0:T(8,128)(2,1)S(1)} all-gather(bf16[32,256]{1,0:T(8,128)(2,1)S(1)} %copy-done.63), channel_id=1, replica_groups=mesh['dp'=16,'mp'=2] {'dp'}, dimensions={0}, use_global_device_ids=true | all-gather | bytes 278528 | tf_op jit(solution)/shard_map/all_gather | solution.py:131
  132.7 3.2 copy.278
  159.6 3.2 copy.294
  162.9 2.8 reshape_reshape.46
  168.2 19.6 %all_gather.21 = bf16[256,512]{0,1:T(8,128)(2,1)} all-gather(bf16[256,32]{0,1:T(8,128)(2,1)S(1)} %copy-done.64), channel_id=1, replica_groups=mesh['dp'=16,'mp'=2] {'dp'}, dimensions={1}, use_global_device_ids=true | all-gather | bytes 278528 | tf_op jit(solution)/shard_map/all_gather | solution.py:133
  209.4 40.9 %all-reduce.15.cloned.1.call-done = (f32[392,512]{1,0:T(8,128)}, f32[392,512]{1,0:T(8,128)}) async-done(((f32[392,512]{1,0:T(8,128)}, f32[392,512]{1,0:T(8,128)}), (f32[392,512]{1,0:T(8,128)}, f32[392,512]{1,0:T(8,128)})) %all-reduce.15.cloned.1.call-update) | async-done | bytes 1605648 | tf_op jit(solution)/shard_map/psum | solution.py:172
  253.7 3.1 fusion.85
  256.7 20.5 %all-gather.7.cloned.1.call-done = bf16[1024,512]{0,1:T(8,128)(2,1)} async-done(((bf16[1024,32]{0,1:T(8,128)(2,1)}), bf16[1024,512]{0,1:T(8,128)(2,1)}) %all-gather.7.cloned.1.call-update) | async-done | bytes 1048592 | tf_op jit(solution)/shard_map/all_gather | solution.py:135
  277.2 3.5 convert_reduce_fusion
  283.2 9.1 %fusion.4 = (bf16[392,1024]{1,0:T(8,128)(2,1)}, bf16[392,1024]{1,0:T(8,128)(2,1)}, f32[392,1024]{1,0:T(8,128)S(1)}) fusion(f32[1024]{0:T(1024)S(1)} %convert_element_type.258, f32[392,1024]{1,0:T(8,128)S(1)} %copy-done.43, bf16[512,1024]{1,0:T(8,128)(2,1)S(1)} %copy-done.44, f32[392,512]{1,0:T(8,128)S(1)} %copy-done.8, f32[512]{0:T(512)S(1)} %bitcast.236, ...), kind=kOutput, calls=%fused_computation.22 | convolution fusion | flops 465031168 | bytes 6679616 | tf_op jit(solution)/shard_map/dot_general | solution.py:176
  296.5 3.0 convolution_convert_fusion.5
  309.3 38.5 %all-reduce.13.cloned.1.call-done = (f32[392,512]{1,0:T(8,128)}, f32[392,512]{1,0:T(8,128)}) async-done(((f32[392,512]{1,0:T(8,128)}, f32[392,512]{1,0:T(8,128)}), (f32[392,512]{1,0:T(8,128)}, f32[392,512]{1,0:T(8,128)})) %all-reduce.13.cloned.1.call-update) | async-done | bytes 1605648 | tf_op jit(solution)/shard_map/psum | solution.py:203
  347.8 3.1 multiply_reduce_fusion.4
  350.9 34.0 %all-reduce.17.cloned.1.call-done = (bf16[392,512]{1,0:T(8,128)(2,1)}, bf16[392,512]{1,0:T(8,128)(2,1)}) async-done(((bf16[392,512]{1,0:T(8,128)(2,1)}, bf16[392,512]{1,0:T(8,128)(2,1)}), (bf16[392,512]{1,0:T(8,128)(2,1)}, bf16[392,512]{1,0:T(8,128)(2,1)})) %all-reduce.17.cloned.1.call-update) | async-done | bytes 802832 | tf_op jit(solution)/shard_map/psum | solution.py:179
  385.0 4.3 fusion.88
  404.7 2.8 copy.300
  407.5 3.1 convert_reduce_fusion.4
  410.7 2.7 multiply_reduce_fusion.1
  416.9 2.8 copy.317
  419.7 3.1 convert_reduce_fusion.2
  480.7 3.0 convert_reduce_fusion.6
  504.2 61.3 %all-reduce.1 = (f32[2,256]{1,0:T(2,128)}, f32[1024]{0:T(1024)}, f32[8,169]{1,0:T(8,128)}) all-reduce(f32[2,256]{1,0:T(2,128)S(1)} %maximum_add_fusion, f32[1024]{0:T(1024)S(1)} %add.504, f32[8,169]{1,0:T(8,128)S(1)} %fusion.56), channel_id=1, replica_groups=mesh['dp'=16,'mp'=2] {'dp'}, use_global_device_ids=true, to_apply=%region_54.55 | all-reduce | flops 2888 | bytes 23104 | tf_op jit(solution)/shard_map/psum | solution.py:311
  568.1 51.5 %reduce-scatter.13.cloned.1.call-done = bf16[32,256]{1,0:T(8,128)(2,1)} async-done(((bf16[512,256]{1,0:T(8,128)(2,1)}), bf16[32,256]{1,0:T(8,128)(2,1)}) %reduce-scatter.13.cloned.1.call-update) | async-done | bytes 16400 | tf_op jit(solution)/shard_map/reduce_scatter | solution.py:286
  620.9 56.9 %reduce-scatter.15.cloned.1.call-done = bf16[32,256]{1,0:T(8,128)(2,1)} async-done(((bf16[512,256]{1,0:T(8,128)(2,1)}), bf16[32,256]{1,0:T(8,128)(2,1)}) %reduce-scatter.15.cloned.1.call-update) | async-done | bytes 16400 | tf_op jit(solution)/shard_map/reduce_scatter | solution.py:289
  680.8 2.6 multiply_reduce_fusion.2
  688.6 50.8 %reduce-scatter.25.cloned.1.call-done = bf16[32,2]{1,0:T(8,128)(2,1)} async-done(((bf16[512,2]{1,0:T(8,128)(2,1)}), bf16[32,2]{1,0:T(8,128)(2,1)}) %reduce-scatter.25.cloned.1.call-update) | async-done | bytes 144
  740.7 56.8 %reduce-scatter.27.cloned.1.call-done = bf16[32,4]{1,0:T(8,128)(2,1)} async-done(((bf16[512,4]{1,0:T(8,128)(2,1)}), bf16[32,4]{1,0:T(8,128)(2,1)}) %reduce-scatter.27.cloned.1.call-update) | async-done | bytes 272
  (429 shorter events, 201.9 us)
Async XLA Ops:
  8.0 113.9 %copy-start = (bf16[8,169]{1,0:T(8,128)(2,1)S(1)}, bf16[8,169]{1,0:T(8,128)(2,1)}, u32[]{:S(2)}) copy-start(bf16[8,169]{1,0:T(8,128)(2,1)} %param.51) | copy-start | bytes 8116
  8.0 44.3 %copy-start.4 = (bf16[4,196,512]{2,0,1:T(4,128)(2,1)S(1)}, bf16[4,196,512]{2,0,1:T(4,128)(2,1)}, u32[]{:S(2)}) copy-start(bf16[4,196,512]{2,0,1:T(4,128)(2,1)} %param.39) | copy-start | bytes 2408452
  8.0 242.3 %all-reduce.15.cloned.1.call-start = ((), (), s32[]{:S(2)}) async-start(), calls=%async_computation.20 | async-start | bytes 3211264 | tf_op jit(solution)/shard_map/psum | solution.py:172
  57.2 20.1 %copy-start.62 = (bf16[32,256]{1,0:T(8,128)(2,1)S(1)}, bf16[32,256]{1,0:T(8,128)(2,1)}, u32[]{:S(2)}) copy-start(bf16[32,256]{1,0:T(8,128)(2,1)} %param.43) | copy-start | bytes 49156
  77.4 20.8 %copy-start.12 = (bf16[512,256]{1,0:T(8,128)(2,1)}, bf16[512,256]{1,0:T(8,128)(2,1)S(1)}, u32[]{:S(2)}) copy-start(bf16[512,256]{1,0:T(8,128)(2,1)S(1)} %all_gather.19) | copy-start | bytes 786436
  99.4 22.3 %copy-start.56 = (s32[49,49]{1,0:T(8,128)S(1)}, s32[49,49]{1,0:T(8,128)}, u32[]{:S(2)}) copy-start(s32[49,49]{1,0:T(8,128)} %param.53) | copy-start | bytes 28816
  99.4 22.4 %copy-start.71 = (s32[4,49]{1,0:T(4,128)S(1)}, s32[4,49]{1,0:T(4,128)}, u32[]{:S(2)}) copy-start(s32[4,49]{1,0:T(4,128)} %param.52) | copy-start | bytes 2356
  159.6 8.6 %copy-start.64 = (bf16[256,32]{0,1:T(8,128)(2,1)S(1)}, bf16[256,32]{0,1:T(8,128)(2,1)}, u32[]{:S(2)}) copy-start(bf16[256,32]{0,1:T(8,128)(2,1)} %param.44) | copy-start | bytes 49156
  199.6 54.1 %all-gather.5.cloned.1.call-start = ((), (), s32[]{:S(2)}) async-start(), calls=%async_computation.8 | async-start | bytes 1114112 | tf_op jit(solution)/shard_map/all_gather | solution.py:134
  200.2 77.1 %all-gather.7.cloned.1.call-start = ((), (), s32[]{:S(2)}) async-start(), calls=%async_computation.9 | async-start | bytes 1114112 | tf_op jit(solution)/shard_map/all_gather | solution.py:135
  200.8 147.1 %all-reduce.13.cloned.1.call-start = ((), (), s32[]{:S(2)}) async-start(), calls=%async_computation.19 | async-start | bytes 3211264 | tf_op jit(solution)/shard_map/psum | solution.py:203
  283.2 9.2 %copy-start.28 = (bf16[392,512]{1,0:T(8,128)(2,1)S(1)}, bf16[392,512]{1,0:T(8,128)(2,1)}, u32[]{:S(2)}) copy-start(bf16[392,512]{1,0:T(8,128)(2,1)} %reshape.591) | copy-start | bytes 1204228
  283.2 9.2 %copy-start.78 = (bf16[1024,512]{0,1:T(8,128)(2,1)S(1)}, bf16[1024,512]{0,1:T(8,128)(2,1)}, u32[]{:S(2)}) copy-start(bf16[1024,512]{0,1:T(8,128)(2,1)} %all-gather.7.cloned.1.call-done) | copy-start | bytes 3145732
  296.4 88.6 %all-reduce.17.cloned.1.call-start = ((), (), s32[]{:S(2)}) async-start(), calls=%async_computation.21 | async-start | bytes 1605632 | tf_op jit(solution)/shard_map/psum | solution.py:179
  300.8 182.8 %reduce-scatter.21.cloned.1.call-start = ((), (), s32[]{:S(2)}) async-start(), calls=%async_computation.14 | async-start | bytes 1114112 | tf_op jit(solution)/shard_map/reduce_scatter | solution.py:298
  305.3 179.9 %reduce-scatter.23.cloned.1.call-start = ((), (), s32[]{:S(2)}) async-start(), calls=%async_computation.15 | async-start | bytes 1114112 | tf_op jit(solution)/shard_map/reduce_scatter | solution.py:301
  309.3 256.2 %reduce-scatter.19.cloned.1.call-start = ((), (), s32[]{:S(2)}) async-start(), calls=%async_computation.13 | async-start | bytes 278528 | tf_op jit(solution)/shard_map/reduce_scatter | solution.py:295
  347.8 37.1 %copy-start.70 = (f32[1,512]{1,0:T(1,128)S(1)}, f32[1,512]{1,0:T(1,128)}, u32[]{:S(2)}) copy-start(f32[1,512]{1,0:T(1,128)} %get-tuple-element.266) | copy-start | bytes 6148
  385.0 5.2 copy-start.11
  389.2 6.6 copy-start.9
  434.6 6.6 copy-start.33
  447.1 119.6 %reduce-scatter.17.cloned.1.call-start = ((), (), s32[]{:S(2)}) async-start(), calls=%async_computation.12 | async-start | bytes 278528 | tf_op jit(solution)/shard_map/reduce_scatter | solution.py:292
  451.5 4.6 copy-start.15
  451.5 168.1 %reduce-scatter.13.cloned.1.call-start = ((), (), s32[]{:S(2)}) async-start(), calls=%async_computation.10 | async-start | bytes 278528 | tf_op jit(solution)/shard_map/reduce_scatter | solution.py:286
  458.6 219.2 %reduce-scatter.15.cloned.1.call-start = ((), (), s32[]{:S(2)}) async-start(), calls=%async_computation.11 | async-start | bytes 278528 | tf_op jit(solution)/shard_map/reduce_scatter | solution.py:289
  461.1 218.0 %all-reduce.11.cloned.1.call-start = ((), (), s32[]{:S(2)}) async-start(), calls=%async_computation.18 | async-start | bytes 3211264 | tf_op jit(solution)/shard_map/psum | solution.py:277
  475.1 264.2 %reduce-scatter.25.cloned.1.call-start = ((), (), s32[]{:S(2)}) async-start(), calls=%async_computation.16 | async-start | bytes 139264
  491.6 4.5 copy-start.60
  491.6 8.4 %copy-start.67 = (f32[512]{0:T(512)S(1)}, f32[512]{0:T(512)}, u32[]{:S(2)}) copy-start(f32[512]{0:T(512)} %get-tuple-element.271) | copy-start | bytes 6148
  497.8 183.0 %copy-start.69 = (f32[392]{0:T(512)S(1)}, f32[392]{0:T(512)}, u32[]{:S(2)}) copy-start(f32[392]{0:T(512)} %rsqrt.50) | copy-start | bytes 4708
  684.6 112.9 %reduce-scatter.27.cloned.1.call-start = ((), (), s32[]{:S(2)}) async-start(), calls=%async_computation.17 | async-start | bytes 139264
  687.2 111.7 %copy-start.1 = (bf16[8,169]{1,0:T(8,128)(2,1)S(1)}, bf16[8,169]{1,0:T(8,128)(2,1)}, u32[]{:S(2)}) copy-start(bf16[8,169]{1,0:T(8,128)(2,1)} %param.51) | copy-start | bytes 8116
  (63 other events, 152.9 us)
Sparse Core Ops, SparseCore 0:
  199.7 50.5 all-reduce.14
  296.5 51.2 all-reduce.12
  350.2 34.7 all-reduce.16
  475.2 52.2 all-reduce.10
Sparse Core Ops, SparseCore 1:
  202.2 36.1 all-gather.4
  240.4 36.8 all-gather.6
  305.4 56.5 reduce-scatter.20
  365.6 56.6 reduce-scatter.22
  447.2 55.7 reduce-scatter.18
  506.5 54.8 reduce-scatter.16
  564.7 54.8 reduce-scatter.12
  623.0 54.8 reduce-scatter.14
  684.6 54.6 reduce-scatter.24
  742.8 54.6 reduce-scatter.26
where the time goes:
time: 815 us; the launch traced here: 806 us
  waiting for transfers between devices  351 us (43%)
  blocking collectives  179 us (22%)
  local copies, waits for them, and re-layouts  118 us (14%)
  matrix products  90.9 us (11%)
  other arithmetic  49.2 us (6%)
  between operations  17.1 us (2%)
    unnamed x16, waiting for transfers between devices  109 us
    psum x1, blocking collectives, body(): head_sums = lax.psum((table_acc, qv_acc, up_bias_acc), 'dp')  61.3 us
    reduce_scatter x1, waiting for transfers between devices, body(): lax.psum_scatter(acc_key.astype(jnp.bfloat16), 'dp', scatter_dimension=0,...  56.9 us
    reduce_scatter x1, waiting for transfers between devices, body(): lax.psum_scatter(acc_query.astype(jnp.bfloat16), 'dp', scatter_dimension=...  51.5 us
    psum x1, waiting for transfers between devices, body(): branch = lax.psum(projected, 'mp') + shift_rows[2]  40.9 us
    psum x1, waiting for transfers between devices, body(): grad_normed_two = lax.psum(lifted, 'mp')  38.5 us
    psum x1, waiting for transfers between devices, body(): lax.psum(lowered.astype(jnp.bfloat16), 'mp').astype(jnp.float32)  34 us
    all_gather x1, blocking collectives, body(): lax.all_gather(gains, 'dp', axis=1, tiled=True)  23.4 us
  transfers between devices with their start and end apart: 14, of which 8 were waited for; matrix products, arithmetic and copies ran while one was open for 19% of the time, Pallas kernels for 0%

commit v1 on v0

--- a/solution.py
+++ b/solution.py
@@ -169,7 +169,7 @@
         ).reshape(row_count, local_width)
         projected = jnp.dot(token_mixed, full_proj, preferred_element_type=jnp.float32)
         source_rows = source.reshape(row_count, model_width)
-        branch = lax.psum(projected, "mp") + shift_rows[2]
+        branch = jnp.sum(lax.all_gather(projected, "mp"), axis=0) + shift_rows[2]
         middle = source_rows + branch
         normed_two, unit_two, inverse_two = normalize(middle, gain_rows[1], shift_rows[1])
         normed_low = normed_two.astype(jnp.bfloat16)

time: 815 us -> 952 us (1.17)
  waiting for transfers between devices: 351 us -> 484 us
    psum x1, waiting for transfers between devices: 0.01 us -> 53 us  [body(): grad_normed_one = lax.psum(token_terms, 'mp')]
    psum x1 -> x0, waiting for transfers between devices: 40.9 us -> none  [body(): branch = lax.psum(projected, 'mp') + shift_rows[2]]
    reduce_scatter x1, waiting for transfers between devices: 0.01 us -> 38.8 us  [body(): lax.psum_scatter(acc_value.astype(jnp.bfloat16), 'dp', scatter_dimension=...]
    reduce_scatter x1, waiting for transfers between devices: 0.01 us -> 31.3 us  [body(): lax.psum_scatter(acc_down.astype(jnp.bfloat16), 'dp', scatter_dimension=1...]
    all_gather x1, waiting for transfers between devices: 0.03 us -> 28.6 us  [body(): lax.all_gather(w_up, 'dp', axis=0, tiled=True)]
    all_gather x1, waiting for transfers between devices: 20.5 us -> 35.8 us  [body(): lax.all_gather(w_down, 'dp', axis=1, tiled=True)]
    unnamed x16 -> x17, waiting for transfers between devices: 109 us -> 107 us
  transfers between devices with their start and end apart: 14 -> 15, of which waited for: 8 -> 12; matrix products, arithmetic and copies ran while one was open for 19% -> 22% of each run, Pallas kernels for 0% -> 0%
where the time goes in v1:
time: 952 us; the launch traced here: 940 us
  waiting for transfers between devices  484 us (51%)
  blocking collectives  174 us (18%)
  local copies, waits for them, and re-layouts  122 us (13%)
  matrix products  91.6 us (10%)
  other arithmetic  51.8 us (5%)
  between operations  15.6 us (2%)
    unnamed x17, waiting for transfers between devices  107 us
    psum x1, blocking collectives, body(): head_sums = lax.psum((table_acc, qv_acc, up_bias_acc), 'dp')  57.7 us
    reduce_scatter x1, waiting for transfers between devices, body(): lax.psum_scatter(acc_query.astype(jnp.bfloat16), 'dp', scatter_dimension=...  57 us
    reduce_scatter x1, waiting for transfers between devices, body(): lax.psum_scatter(acc_key.astype(jnp.bfloat16), 'dp', scatter_dimension=0,...  56.9 us
    psum x1, waiting for transfers between devices, body(): grad_normed_one = lax.psum(token_terms, 'mp')  53 us
    reduce_scatter x1, waiting for transfers between devices, body(): lax.psum_scatter(acc_value.astype(jnp.bfloat16), 'dp', scatter_dimension=...  38.8 us
    psum x1, waiting for transfers between devices, body(): grad_normed_two = lax.psum(lifted, 'mp')  38.5 us
    all_gather x1, waiting for transfers between devices, body(): lax.all_gather(w_down, 'dp', axis=1, tiled=True)  35.8 us
  transfers between devices with their start and end apart: 15, of which 12 were waited for; matrix products, arithmetic and copies ran while one was open for 22% of the time, Pallas kernels for 0%

profile of v1, /device:TPU:0, one launch (start us, length us, event | category | flops | bytes accessed | tf_op | source)
XLA Modules:
  0.0 940.4 jit_solution(11313384894183692606)
XLA Ops:
  7.2 23.3 %all-gather.2 = bf16[16,32,2]{1,2,0:T(2,128)(2,1)S(1)} all-gather(bf16[1,32,2]{1,2,0:T(2,128)(2,1)} %bitcast.271), channel_id=1, replica_groups=mesh['dp'=16,'mp'=2] {'dp'}, dimensions={0}, use_global_device_ids=true | all-gather | bytes 2176 | tf_op jit(solution)/shard_map/all_gather | solution.py:136
  30.6 17.7 %all-gather.3 = bf16[16,32,4]{1,2,0:T(4,128)(2,1)S(1)} all-gather(bf16[1,32,4]{1,2,0:T(4,128)(2,1)} %bitcast.270), channel_id=1, replica_groups=mesh['dp'=16,'mp'=2] {'dp'}, dimensions={0}, use_global_device_ids=true | all-gather | bytes 4352 | tf_op jit(solution)/shard_map/all_gather | solution.py:137
  55.0 19.4 %all_gather.27 = bf16[512,256]{1,0:T(8,128)(2,1)S(1)} all-gather(bf16[32,256]{1,0:T(8,128)(2,1)S(1)} %copy-done.58), channel_id=1, replica_groups=mesh['dp'=16,'mp'=2] {'dp'}, dimensions={0}, use_global_device_ids=true | all-gather | bytes 278528 | tf_op jit(solution)/shard_map/all_gather | solution.py:130
  74.4 18.2 %all_gather.28 = bf16[512,256]{1,0:T(8,128)(2,1)S(1)} all-gather(bf16[32,256]{1,0:T(8,128)(2,1)S(1)} %copy-done.59), channel_id=1, replica_groups=mesh['dp'=16,'mp'=2] {'dp'}, dimensions={0}, use_global_device_ids=true | all-gather | bytes 278528 | tf_op jit(solution)/shard_map/all_gather | solution.py:131
  92.6 19.4 %all_gather.26 = bf16[512,256]{1,0:T(8,128)(2,1)S(1)} all-gather(bf16[32,256]{1,0:T(8,128)(2,1)S(1)} %copy-done.60), channel_id=1, replica_groups=mesh['dp'=16,'mp'=2] {'dp'}, dimensions={0}, use_global_device_ids=true | all-gather | bytes 278528 | tf_op jit(solution)/shard_map/all_gather | solution.py:132
  123.5 3.2 copy.265
  128.8 18.4 %all_gather.29 = bf16[256,512]{0,1:T(8,128)(2,1)S(1)} all-gather(bf16[256,32]{0,1:T(8,128)(2,1)S(1)} %copy-done.61), channel_id=1, replica_groups=mesh['dp'=16,'mp'=2] {'dp'}, dimensions={1}, use_global_device_ids=true | all-gather | bytes 278528 | tf_op jit(solution)/shard_map/all_gather | solution.py:133
  181.9 3.2 copy.278
  216.1 3.6 all-gather.15.cloned.1.call-done
  228.0 3.2 add_add_fusion.5
  231.2 28.6 %all-gather.9.cloned.1.call-done = bf16[512,1024]{1,0:T(8,128)(2,1)} async-done(((bf16[32,1024]{1,0:T(8,128)(2,1)}), bf16[512,1024]{1,0:T(8,128)(2,1)}) %all-gather.9.cloned.1.call-update) | async-done | bytes 1048592 | tf_op jit(solution)/shard_map/all_gather | solution.py:134
  259.8 3.1 fusion.87
  262.9 35.8 %all-gather.11.cloned.1.call-done = bf16[1024,512]{0,1:T(8,128)(2,1)} async-done(((bf16[1024,32]{0,1:T(8,128)(2,1)}), bf16[1024,512]{0,1:T(8,128)(2,1)}) %all-gather.11.cloned.1.call-update) | async-done | bytes 1048592 | tf_op jit(solution)/shard_map/all_gather | solution.py:135
  298.7 3.5 convert_reduce_fusion
  304.5 9.1 fusion.4
  317.7 3.0 convolution_convert_fusion.5
  330.6 38.5 %all-reduce.11.cloned.1.call-done = (f32[392,512]{1,0:T(8,128)}, f32[392,512]{1,0:T(8,128)}) async-done(((f32[392,512]{1,0:T(8,128)}, f32[392,512]{1,0:T(8,128)}), (f32[392,512]{1,0:T(8,128)}, f32[392,512]{1,0:T(8,128)})) %all-reduce.11.cloned.1.call-update) | async-done | bytes 1605648 | tf_op jit(solution)/shard_map/psum | solution.py:203
  369.1 3.1 multiply_reduce_fusion.8
  372.1 33.9 %all-reduce.13.cloned.1.call-done = (bf16[392,512]{1,0:T(8,128)(2,1)}, bf16[392,512]{1,0:T(8,128)(2,1)}) async-done(((bf16[392,512]{1,0:T(8,128)(2,1)}, bf16[392,512]{1,0:T(8,128)(2,1)}), (bf16[392,512]{1,0:T(8,128)(2,1)}, bf16[392,512]{1,0:T(8,128)(2,1)})) %all-reduce.13.cloned.1.call-update) | async-done | bytes 802832 | tf_op jit(solution)/shard_map/psum | solution.py:179
  406.0 4.3 fusion.90
  425.7 2.8 copy.284
  436.6 2.8 copy.300
  439.5 3.1 convert_reduce_fusion.2
  496.2 31.3 %reduce-scatter.23.cloned.1.call-done = bf16[1024,32]{0,1:T(8,128)(2,1)} async-done(((bf16[1024,512]{0,1:T(8,128)(2,1)}), bf16[1024,32]{0,1:T(8,128)(2,1)}) %reduce-scatter.23.cloned.1.call-update) | async-done | bytes 65552 | tf_op jit(solution)/shard_map/reduce_scatter | solution.py:301
  546.2 57.7 %all-reduce.1 = (f32[2,256]{1,0:T(2,128)}, f32[1024]{0:T(1024)}, f32[8,169]{1,0:T(8,128)}) all-reduce(f32[2,256]{1,0:T(2,128)S(1)} %maximum_add_fusion, f32[1024]{0:T(1024)S(1)} %add.525, f32[8,169]{1,0:T(8,128)S(1)} %fusion.56), channel_id=1, replica_groups=mesh['dp'=16,'mp'=2] {'dp'}, use_global_device_ids=true, to_apply=%region_54.55 | all-reduce | flops 2888 | bytes 23104 | tf_op jit(solution)/shard_map/psum | solution.py:311
  605.3 38.8 %reduce-scatter.17.cloned.1.call-done = bf16[32,256]{1,0:T(8,128)(2,1)} async-done(((bf16[512,256]{1,0:T(8,128)(2,1)}), bf16[32,256]{1,0:T(8,128)(2,1)}) %reduce-scatter.17.cloned.1.call-update) | async-done | bytes 16400 | tf_op jit(solution)/shard_map/reduce_scatter | solution.py:292
  645.4 57.0 %reduce-scatter.13.cloned.1.call-done = bf16[32,256]{1,0:T(8,128)(2,1)} async-done(((bf16[512,256]{1,0:T(8,128)(2,1)}), bf16[32,256]{1,0:T(8,128)(2,1)}) %reduce-scatter.13.cloned.1.call-update) | async-done | bytes 16400 | tf_op jit(solution)/shard_map/reduce_scatter | solution.py:286
  703.8 56.9 %reduce-scatter.15.cloned.1.call-done = bf16[32,256]{1,0:T(8,128)(2,1)} async-done(((bf16[512,256]{1,0:T(8,128)(2,1)}), bf16[32,256]{1,0:T(8,128)(2,1)}) %reduce-scatter.15.cloned.1.call-update) | async-done | bytes 16400 | tf_op jit(solution)/shard_map/reduce_scatter | solution.py:289
  762.0 53.0 %all-reduce.9.cloned.1.call-done = (f32[392,512]{1,0:T(8,128)}, f32[392,512]{1,0:T(8,128)}) async-done(((f32[392,512]{1,0:T(8,128)}, f32[392,512]{1,0:T(8,128)}), (f32[392,512]{1,0:T(8,128)}, f32[392,512]{1,0:T(8,128)})) %all-reduce.9.cloned.1.call-update) | async-done | bytes 1605648 | tf_op jit(solution)/shard_map/psum | solution.py:277
  818.4 2.7 add_convert_fusion.5
  825.5 48.5 %reduce-scatter.25.cloned.1.call-done = bf16[32,2]{1,0:T(8,128)(2,1)} async-done(((bf16[512,2]{1,0:T(8,128)(2,1)}), bf16[32,2]{1,0:T(8,128)(2,1)}) %reduce-scatter.25.cloned.1.call-update) | async-done | bytes 144
  875.4 56.6 %reduce-scatter.27.cloned.1.call-done = bf16[32,4]{1,0:T(8,128)(2,1)} async-done(((bf16[512,4]{1,0:T(8,128)(2,1)}), bf16[32,4]{1,0:T(8,128)(2,1)}) %reduce-scatter.27.cloned.1.call-update) | async-done | bytes 272
  (433 shorter events, 220.9 us)
Async XLA Ops:
  7.2 46.4 %copy-start = (bf16[8,169]{1,0:T(8,128)(2,1)S(1)}, bf16[8,169]{1,0:T(8,128)(2,1)}, u32[]{:S(2)}) copy-start(bf16[8,169]{1,0:T(8,128)(2,1)} %param.51) | copy-start | bytes 8116
  7.2 202.9 %all-gather.13.cloned.1.call-start = ((), (), s32[]{:S(2)}) async-start(), calls=%async_computation.16 | async-start | bytes 2408448 | tf_op jit(solution)/shard_map/all_gather | solution.py:172
  52.7 21.7 %copy-start.59 = (bf16[32,256]{1,0:T(8,128)(2,1)S(1)}, bf16[32,256]{1,0:T(8,128)(2,1)}, u32[]{:S(2)}) copy-start(bf16[32,256]{1,0:T(8,128)(2,1)} %param.42) | copy-start | bytes 49156
  52.7 39.9 %copy-start.60 = (bf16[32,256]{1,0:T(8,128)(2,1)S(1)}, bf16[32,256]{1,0:T(8,128)(2,1)}, u32[]{:S(2)}) copy-start(bf16[32,256]{1,0:T(8,128)(2,1)} %param.43) | copy-start | bytes 49156
  53.5 39.1 %copy-start.62 = (s32[2401]{0:T(1024)}, s32[2401]{0:T(1024)S(1)}, u32[]{:S(2)}) copy-start(s32[2401]{0:T(1024)S(1)} %eq.35) | copy-start | bytes 28816
  74.4 42.7 %copy-start.11 = (bf16[512,256]{1,0:T(8,128)(2,1)}, bf16[512,256]{1,0:T(8,128)(2,1)S(1)}, u32[]{:S(2)}) copy-start(bf16[512,256]{1,0:T(8,128)(2,1)S(1)} %all_gather.27) | copy-start | bytes 786436
  92.6 20.6 %copy-start.15 = (bf16[512,256]{1,0:T(8,128)(2,1)}, bf16[512,256]{1,0:T(8,128)(2,1)S(1)}, u32[]{:S(2)}) copy-start(bf16[512,256]{1,0:T(8,128)(2,1)S(1)} %all_gather.28) | copy-start | bytes 786436
  123.5 5.3 copy-start.61
  147.2 4.8 copy-start.9
  152.0 67.7 %all-gather.15.cloned.1.call-start = ((), (), s32[]{:S(2)}) async-start(), calls=%async_computation.17 | async-start | bytes 2408448 | tf_op jit(solution)/shard_map/all_gather | solution.py:172
  193.7 66.1 %all-gather.9.cloned.1.call-start = ((), (), s32[]{:S(2)}) async-start(), calls=%async_computation.8 | async-start | bytes 1114112 | tf_op jit(solution)/shard_map/all_gather | solution.py:134
  194.4 104.3 %all-gather.11.cloned.1.call-start = ((), (), s32[]{:S(2)}) async-start(), calls=%async_computation.9 | async-start | bytes 1114112 | tf_op jit(solution)/shard_map/all_gather | solution.py:135
  195.0 174.0 %all-reduce.11.cloned.1.call-start = ((), (), s32[]{:S(2)}) async-start(), calls=%async_computation.21 | async-start | bytes 3211264 | tf_op jit(solution)/shard_map/psum | solution.py:203
  259.8 38.9 %copy-start.71 = (f32[1024]{0:T(1024)S(1)}, f32[1024]{0:T(1024)}, u32[]{:S(2)}) copy-start(f32[1024]{0:T(1024)} %convert_element_type.258) | copy-start | bytes 12292
  304.5 9.1 copy-start.27
  304.5 9.1 copy-start.74
  317.7 88.4 %all-reduce.13.cloned.1.call-start = ((), (), s32[]{:S(2)}) async-start(), calls=%async_computation.22 | async-start | bytes 1605632 | tf_op jit(solution)/shard_map/psum | solution.py:179
  322.1 172.6 %reduce-scatter.21.cloned.1.call-start = ((), (), s32[]{:S(2)}) async-start(), calls=%async_computation.14 | async-start | bytes 1114112 | tf_op jit(solution)/shard_map/reduce_scatter | solution.py:298
  326.5 201.0 %reduce-scatter.23.cloned.1.call-start = ((), (), s32[]{:S(2)}) async-start(), calls=%async_computation.15 | async-start | bytes 1114112 | tf_op jit(solution)/shard_map/reduce_scatter | solution.py:301
  330.5 273.4 %reduce-scatter.19.cloned.1.call-start = ((), (), s32[]{:S(2)}) async-start(), calls=%async_computation.13 | async-start | bytes 278528 | tf_op jit(solution)/shard_map/reduce_scatter | solution.py:295
  406.0 5.2 copy-start.10
  410.3 6.5 copy-start.6
  454.1 6.6 copy-start.34
  466.6 177.5 %reduce-scatter.17.cloned.1.call-start = ((), (), s32[]{:S(2)}) async-start(), calls=%async_computation.12 | async-start | bytes 278528 | tf_op jit(solution)/shard_map/reduce_scatter | solution.py:292
  471.0 4.6 copy-start.14
  471.0 231.4 %reduce-scatter.13.cloned.1.call-start = ((), (), s32[]{:S(2)}) async-start(), calls=%async_computation.10 | async-start | bytes 278528 | tf_op jit(solution)/shard_map/reduce_scatter | solution.py:286
  478.2 282.5 %reduce-scatter.15.cloned.1.call-start = ((), (), s32[]{:S(2)}) async-start(), calls=%async_computation.11 | async-start | bytes 278528 | tf_op jit(solution)/shard_map/reduce_scatter | solution.py:289
  479.8 335.2 %all-reduce.9.cloned.1.call-start = ((), (), s32[]{:S(2)}) async-start(), calls=%async_computation.20 | async-start | bytes 3211264 | tf_op jit(solution)/shard_map/psum | solution.py:277
  490.6 383.4 %reduce-scatter.25.cloned.1.call-start = ((), (), s32[]{:S(2)}) async-start(), calls=%async_computation.18 | async-start | bytes 139264
  534.0 5.8 copy-start.55
  818.3 113.7 %reduce-scatter.27.cloned.1.call-start = ((), (), s32[]{:S(2)}) async-start(), calls=%async_computation.19 | async-start | bytes 139264
  824.2 109.3 %copy-start.1 = (bf16[8,169]{1,0:T(8,128)(2,1)S(1)}, bf16[8,169]{1,0:T(8,128)(2,1)}, u32[]{:S(2)}) copy-start(bf16[8,169]{1,0:T(8,128)(2,1)} %param.51) | copy-start | bytes 8116
  (60 other events, 135.8 us)
Sparse Core Ops, SparseCore 0:
  152.1 25.8 all-gather.12
  193.8 25.8 all-gather.14
  221.9 37.8 all-gather.8
  261.9 36.8 all-gather.10
  317.8 51.2 all-reduce.10
  371.3 34.7 all-reduce.12
  409.7 57.5 reduce-scatter.20
  470.9 56.6 reduce-scatter.22
  531.1 54.8 reduce-scatter.18
  589.3 54.7 reduce-scatter.16
  647.6 54.7 reduce-scatter.12
  705.8 54.7 reduce-scatter.14
  763.6 51.3 all-reduce.8
  818.4 55.5 reduce-scatter.24
  877.4 54.6 reduce-scatter.26
